TPU v7x, 32 devices: a whole 2x2x4 slice. The times are simulated.
32 devices in a mesh: occ: 8 (over z, y), aux: 4 (over x, core).
Axes of the slice: x: 2, y: 2, z: 4, core: 2. Of those that a mesh axis runs over, the one named last changes fastest.
Arguments:
- b_alpha: bfloat16 [16, 512, 1536], P('occ', None, 'aux'), may hold values from -0.95703125 to 0.95703125
- b_beta: bfloat16 [16, 512, 1536], P('occ', None, 'aux'), may hold values from -0.95703125 to 0.95703125
- eps_occ_alpha: float32 [16], replicated, may hold values from -3 to -0.3
- eps_occ_beta: float32 [16], replicated, may hold values from -3 to -0.3
- eps_vir_alpha: float32 [512], replicated, may hold values from 0.2 to 4
- eps_vir_beta: float32 [512], replicated, may hold values from 0.2 to 4
- row_orbital: int32 [16], replicated, may hold values from 0 to 15, as said below
- pair_list: int32 [4, 8, 2], replicated, may hold values from 0 to 15, as said below
- live_mask: int32 [4, 8], replicated, may hold values 0 or 1
Outputs:
- gamma_alpha: float32 [16, 512, 1536], P('occ', None, 'aux')
- gamma_beta: float32 [16, 512, 1536], P('occ', None, 'aux')
Inputs may be any that keep to these rules, and one draw needn't show every extreme that they name: A permutation: stored row r of b_alpha, b_beta and the outputs belongs to occupied orbital row_orbital[r]. `pair_list`: for slot s and worker w the entry (i, j) has r(i) among the stored rows w * 2 to (w + 1) * 2 - 1 and r(j) among the stored rows of worker (w - d) mod 8, where d = 1 + s * (8 // 4) and r is the inverse of row_orbital.
All inputs are finite; a program needn't handle non-finite values.
Results may differ from a plain program's by a relative error of at most 0.01.
Values may be sent and summed in bfloat16 or wider, within the bound.
A program may use at most 64 MiB of HBM per device.

v0:
```python
import jax
import jax.numpy as jnp
from jax import lax
from jax.sharding import PartitionSpec as P


def passed_along(block, axis, distance):
    devices = range(lax.axis_size(axis))
    route = [((i - distance) % len(devices), i) for i in devices]
    return lax.ppermute(block, axis, route)


def lookup(values_table, orbital):
    places = jnp.arange(values_table.shape[0], dtype=jnp.int32)
    return jnp.sum(jnp.where(places == orbital, values_table, jnp.zeros_like(values_table)))


def stored_row(row_orbital, orbital):
    places = jnp.arange(row_orbital.shape[0], dtype=jnp.int32)
    return jnp.sum(jnp.where(row_orbital == orbital, places, 0))


def add_row(totals, row_index, row_term):
    current = lax.dynamic_index_in_dim(totals, row_index, 0, keepdims=False)
    return lax.dynamic_update_index_in_dim(totals, current + row_term, row_index, 0)


def shards(
    b_alpha,
    b_beta,
    eps_occ_alpha,
    eps_occ_beta,
    eps_vir_alpha,
    eps_vir_beta,
    row_orbital,
    pair_list,
    live_mask,
):
    workers = lax.axis_size("occ")
    worker = lax.axis_index("occ")
    local_rows = b_alpha.shape[0]
    slot_count = pair_list.shape[0]
    contract = (((1,), (1,)), ((), ()))
    gamma_alpha = jnp.zeros(b_alpha.shape, jnp.float32)
    gamma_beta = jnp.zeros(b_beta.shape, jnp.float32)
    for slot_index in range(slot_count):
        distance = 1 + slot_index * (workers // slot_count)
        entries = pair_list[slot_index]
        own_pair = lax.dynamic_index_in_dim(entries, worker, 0, keepdims=False)
        label_i = own_pair[0]
        label_j = own_pair[1]
        live_flag = lax.dynamic_index_in_dim(
            live_mask[slot_index], worker, 0, keepdims=False
        ).astype(jnp.float32)
        row_i = stored_row(row_orbital, label_i) - worker * local_rows
        block_i = lax.dynamic_index_in_dim(b_alpha, row_i, 0, keepdims=False)
        partner = jnp.mod(worker + distance, workers)
        wanted = lax.dynamic_index_in_dim(entries, partner, 0, keepdims=False)[1]
        row_out = stored_row(row_orbital, wanted) - worker * local_rows
        block_out = lax.dynamic_index_in_dim(b_beta, row_out, 0, keepdims=False)
        block_j = passed_along(block_out, "occ", distance)
        energy_gap = (
            eps_vir_alpha[:, None]
            + eps_vir_beta[None, :]
            - lookup(eps_occ_alpha, label_i)
            - lookup(eps_occ_beta, label_j)
        )
        partial_values = lax.dot_general(
            block_i, block_j, contract, preferred_element_type=jnp.float32
        )
        integrals = lax.psum(partial_values.astype(jnp.bfloat16), "aux").astype(jnp.float32)
        amplitude = (live_flag * integrals / energy_gap).astype(jnp.bfloat16)
        term_alpha = jnp.dot(amplitude, block_j, preferred_element_type=jnp.float32)
        term_beta = lax.dot_general(
            amplitude, block_i, (((0,), (0,)), ((), ())), preferred_element_type=jnp.float32
        )
        gamma_alpha = add_row(gamma_alpha, row_i, term_alpha)
        returned = passed_along(term_beta.astype(jnp.bfloat16), "occ", -distance).astype(
            term_beta.dtype
        )
        label_back = lax.dynamic_index_in_dim(entries, partner, 0, keepdims=False)[1]
        row_back = stored_row(row_orbital, label_back) - worker * local_rows
        gamma_beta = add_row(gamma_beta, row_back, returned)
    return (gamma_alpha, gamma_beta)


def solution(mesh):
    placed = (P("occ", None, "aux"), P("occ", None, "aux"), P(), P(), P(), P(), P(), P(), P())
    return jax.shard_map(
        shards,
        mesh=mesh,
        in_specs=placed,
        out_specs=(P("occ", None, "aux"), P("occ", None, "aux")),
        check_vma=False,
    )
```

profile of v0, /device:TPU:0, one launch (start us, length us, event | category | flops | bytes accessed | tf_op | source)
XLA Modules:
  0.0 179.5 jit_solution(8348753327962137700)
XLA Ops:
  7.3 0.8 fusion.70
  8.1 0.1 constant_dynamic-slice_fusion.6
  8.1 0.5 slice.94
  8.7 0.5 slice.89
  9.2 0.5 fusion.72
  9.7 0.1 constant_dynamic-slice_fusion.14
  9.7 0.6 slice.84
  10.3 0.6 fusion.74
  10.9 0.5 slice.79
  11.4 0.6 fusion.73
  12.0 0.5 fusion.75
  12.5 6.5 %fusion.50 = (s32[]{:T(128)}, s32[]{:T(128)}, s32[]{:T(128)}, s32[]{:T(128)}, s32[]{:T(128)}, /*index=5*/s32[]{:T(128)}, s32[]{:T(128)}, s32[]{:T(128)}) fusion(s32[16]{0:T(128)} %param.15, s32[]{:T(128)} %bitcast.27, s32[]{:T(128)} %bitcast.19, s32[]{:T(128)} %bitcast.15, s32[]{:T(128)} %bitcast.11, s32[]{:T(128)} %bitcast.7, s32[]{:T(128)} %bitcast.3, ...), kind=kLoop, calls=%fused_computation.114 | loop fusion | flops 376 | bytes 128 | tf_op jit(solution)/shard_map/reduce_sum | solution.py:20
  21.6 2.5 %dynamic-slice_bitcast_fusion = (bf16[512,384]{1,0:T(8,128)(2,1)S(1)}, bf16[512,384]{1,0:T(8,128)(2,1)S(1)}, bf16[512,384]{1,0:T(8,128)(2,1)}, bf16[512,384]{1,0:T(8,128)(2,1)S(1)}) fusion(bf16[2,512,384]{2,1,0:T(8,128)(2,1)} %param.10, s32[]{:T(128)S(6)} %select_n.174, s32[]{:T(128)S(6)} %select_n.158, s32[]{:T(128)S(6)} %select_n.150, s32[]{:T(128)S(6)} %select_n.166), kind=kLoop, calls=%fused_computation.47 | loop fusion | bytes 3145744 | tf_op jit(solution)/shard_map/jit(dynamic_index_in_dim)/squeeze | solution.py:60
  24.1 2.8 %collective-permute-start = (bf16[512,384]{1,0:T(8,128)(2,1)}, bf16[512,384]{1,0:T(8,128)(2,1)S(1)}, u32[]{:S(2)}, u32[]{:S(2)}) collective-permute-start(bf16[512,384]{1,0:T(8,128)(2,1)} %get-tuple-element.24), channel_id=1, source_target_pairs={{28,0},{0,4},{4,8},{8,12},{12,16},{16,20},{20,24},{24,28},{29,1},{... | collective-permute-start | bytes 1179656 | tf_op jit(solution)/shard_map/ppermute | solution.py:10
  26.9 2.6 %collective-permute-start.1 = (bf16[512,384]{1,0:T(8,128)(2,1)S(1)}, bf16[512,384]{1,0:T(8,128)(2,1)S(1)}, u32[]{:S(2)}, u32[]{:S(2)}) collective-permute-start(bf16[512,384]{1,0:T(8,128)(2,1)S(1)} %get-tuple-element.23), channel_id=1, source_target_pairs={{20,0},{24,4},{28,8},{0,12},{4,16},{8,20},{12,24},{16,28},{21,1},{... | collective-permute-start | bytes 1179656 | tf_op jit(solution)/shard_map/ppermute | solution.py:10
  29.6 1.2 collective-permute-start.2
  30.8 2.1 %collective-permute-start.3 = (bf16[512,384]{1,0:T(8,128)(2,1)S(1)}, bf16[512,384]{1,0:T(8,128)(2,1)S(1)}, u32[]{:S(2)}, u32[]{:S(2)}) collective-permute-start(bf16[512,384]{1,0:T(8,128)(2,1)S(1)} %get-tuple-element.22), channel_id=1, source_target_pairs={{4,0},{8,4},{12,8},{16,12},{20,16},{24,20},{28,24},{0,28},{5,1},{9... | collective-permute-start | bytes 1179656 | tf_op jit(solution)/shard_map/ppermute | solution.py:10
  35.3 25.6 %collective-permute-done = bf16[512,384]{1,0:T(8,128)(2,1)S(1)} collective-permute-done((bf16[512,384]{1,0:T(8,128)(2,1)}, bf16[512,384]{1,0:T(8,128)(2,1)S(1)}, u32[]{:S(2)}, u32[]{:S(2)}) %collective-permute-start) | collective-permute-done | bytes 393248 | tf_op jit(solution)/shard_map/ppermute | solution.py:10
  60.9 1.3 convolution_convert_fusion.3
  62.2 1.3 convolution_convert_fusion.2
  63.4 1.3 convolution_convert_fusion.1
  64.7 1.3 convolution_convert_fusion
  66.1 0.7 fusion.76
  66.7 0.6 fusion.78
  67.3 3.1 %fusion.51 = (f32[]{:T(128)}, f32[]{:T(128)}, f32[]{:T(128)}, f32[]{:T(128)}) fusion(f32[16]{0:T(128)S(1)} %copy-done.4, s32[]{:T(128)} %bitcast.23, s32[]{:T(128)} %bitcast.7, s32[]{:T(128)} %bitcast.1, s32[]{:T(128)} %bitcast.15), kind=kLoop, calls=%fused_computation.115 | loop fusion | flops 188 | bytes 96 | tf_op jit(solution)/shard_map/reduce_sum | solution.py:15
  70.4 3.1 %fusion.52 = (f32[]{:T(128)}, f32[]{:T(128)}, f32[]{:T(128)}, f32[]{:T(128)}) fusion(f32[16]{0:T(128)S(1)} %copy-done.5, s32[]{:T(128)} %bitcast.29, s32[]{:T(128)} %bitcast.13, s32[]{:T(128)} %bitcast.5, s32[]{:T(128)} %bitcast.21), kind=kLoop, calls=%fused_computation.116 | loop fusion | flops 188 | bytes 96 | tf_op jit(solution)/shard_map/reduce_sum | solution.py:15
  73.5 45.7 %all-reduce.3.cloned.1.call-done = (bf16[512,512]{1,0:T(8,128)(2,1)}, bf16[512,512]{1,0:T(8,128)(2,1)}, bf16[512,512]{1,0:T(8,128)(2,1)}, bf16[512,512]{1,0:T(8,128)(2,1)}) async-done(((bf16[512,512]{1,0:T(8,128)(2,1)}, bf16[512,512]{1,0:T(8,128)(2,1)}, bf16[512,512]{1,0:T(8,128)(2,1)}, bf16[512,512]{1,0:T(8,128)(2,1)}), (bf16[512,512]{1,0:T(8,128)(2,1)}, bf16[512,512]{1,0:T(8,128)(2,1)}, ...) | async-done | bytes 2097168 | tf_op jit(solution)/shard_map/psum | solution.py:71
  119.3 3.5 %convolution_convert_fusion.7 = bf16[512,384]{1,0:T(8,128)(2,1)S(1)} fusion(bf16[2,512,384]{2,1,0:T(8,128)(2,1)S(1)} %copy-done, s32[]{:T(128)S(6)} %select_n.146, bf16[512,512]{1,0:T(8,128)(2,1)} %get-tuple-element.18, f32[]{:T(128)} %get-tuple-element.8, f32[]{:T(128)} %get-tuple-element.4, f32[512]{0:T(512)S(1)} %copy-done.10, f32[512]{0:T(512)S(1)} %copy-done.11, ...), kind=kOutput, calls=%fused_computation.13 | convolution fusion | flops 203358208 | bytes 1314832 | tf_op jit(solution)/shard_map/dot_general | solution.py:74
  122.8 0.1 broadcast.17.clone
  122.9 0.9 copy-done.9
  123.8 2.3 %fusion = f32[2,512,384]{2,1,0:T(8,128)S(1)} fusion(f32[2,512,384]{2,1,0:T(8,128)S(1)} %broadcast.17.clone, s32[]{:T(128)S(6)} %select_n.146, bf16[512,384]{1,0:T(8,128)(2,1)S(1)} %collective-permute-done, bf16[512,512]{1,0:T(8,128)(2,1)S(1)} %copy-done.9, f32[]{:T(128)} %get-tuple-element.8, f32[]{:T(128)} %get-tuple-element.4, f32[512]{0:T(512)S(1)} %copy-done.10, ...), kind=kOutput, calls=%fused_computation.8 | convolution fusion | flops 203161600 | bytes 1708048 | tf_op jit(solution)/shard_map/dot_general | solution.py:73
  126.2 1.0 copy-done.8
  127.2 2.6 %convolution_convert_fusion.6 = bf16[512,384]{1,0:T(8,128)(2,1)S(1)} fusion(bf16[2,512,384]{2,1,0:T(8,128)(2,1)S(1)} %copy-done, s32[]{:T(128)S(6)} %select_n.154, bf16[512,512]{1,0:T(8,128)(2,1)S(1)} %copy-done.8, f32[]{:T(128)} %get-tuple-element.7, f32[]{:T(128)} %get-tuple-element.3, f32[]{:T(128)} %bitcast.9, f32[512]{0:T(512)S(1)} %copy-done.10, ...), kind=kOutput, calls=%fused_computation.12 | convolution fusion | flops 203358208 | bytes 1314832 | tf_op jit(solution)/shard_map/dot_general | solution.py:74
  129.8 2.5 %bitcast_dynamic-update-slice_fusion.5 = f32[2,512,384]{2,1,0:T(8,128)S(1)} fusion(f32[2,512,384]{2,1,0:T(8,128)S(1)} %fusion, s32[]{:T(128)S(6)} %select_n.154, f32[1,512,384]{2,1,0:T(8,128)S(1)} %constant_dynamic-slice_fusion.13, bf16[512,384]{1,0:T(8,128)(2,1)S(1)} %collective-permute-done.1, bf16[512,512]{1,0:T(8,128)(2,1)S(1)} %copy-done.8, ...), kind=kOutput, calls=%fused_computation.37 | convolution fusion | flops 203358208 | bytes 2494480 | tf_op jit(solution)/shard_map/dot_general | solution.py:73
  132.4 4.3 %collective-permute-start.4 = (bf16[512,384]{1,0:T(8,128)(2,1)S(1)}, bf16[512,384]{1,0:T(8,128)(2,1)S(1)}, u32[]{:S(2)}, u32[]{:S(2)}) collective-permute-start(bf16[512,384]{1,0:T(8,128)(2,1)S(1)} %convolution_convert_fusion.7), channel_id=1, source_target_pairs={{4,0},{8,4},{12,8},{16,12},{20,16},{24,20},{28,24},{0,28},{5,1},{9... | collective-permute-start | bytes 1179656 | tf_op jit(solution)/shard_map/ppermute | solution.py:10
  136.7 2.6 %convolution_convert_fusion.5 = bf16[512,384]{1,0:T(8,128)(2,1)S(1)} fusion(bf16[2,512,384]{2,1,0:T(8,128)(2,1)S(1)} %copy-done, s32[]{:T(128)S(6)} %select_n.162, bf16[512,512]{1,0:T(8,128)(2,1)S(1)} %copy-done.7, f32[]{:T(128)} %get-tuple-element.9, f32[]{:T(128)} %get-tuple-element.5, f32[]{:T(128)} %bitcast.17, f32[512]{0:T(512)S(1)} %copy-done.10, ...), kind=kOutput, calls=%fused_computation.11 | convolution fusion | flops 203358208 | bytes 1314832 | tf_op jit(solution)/shard_map/dot_general | solution.py:74
  139.2 3.0 %collective-permute-start.6 = (bf16[512,384]{1,0:T(8,128)(2,1)S(1)}, bf16[512,384]{1,0:T(8,128)(2,1)S(1)}, u32[]{:S(2)}, u32[]{:S(2)}) collective-permute-start(bf16[512,384]{1,0:T(8,128)(2,1)S(1)} %convolution_convert_fusion.5), channel_id=1, source_target_pairs={{20,0},{24,4},{28,8},{0,12},{4,16},{8,20},{12,24},{16,28},{21,1},{... | collective-permute-start | bytes 1179656 | tf_op jit(solution)/shard_map/ppermute | solution.py:10
  142.2 2.4 %convolution_convert_fusion.4 = bf16[512,384]{1,0:T(8,128)(2,1)S(1)} fusion(bf16[2,512,384]{2,1,0:T(8,128)(2,1)S(1)} %copy-done, s32[]{:T(128)S(6)} %select_n.170, bf16[512,512]{1,0:T(8,128)(2,1)S(1)} %copy-done.6, f32[]{:T(128)} %get-tuple-element.6, f32[]{:T(128)} %get-tuple-element.2, f32[]{:T(128)} %bitcast.25, f32[512]{0:T(512)S(1)} %copy-done.10, ...), kind=kOutput, calls=%fused_computation.10 | convolution fusion | flops 203358208 | bytes 1314832 | tf_op jit(solution)/shard_map/dot_general | solution.py:74
  144.7 2.4 %bitcast_dynamic-update-slice_fusion.4 = f32[2,512,384]{2,1,0:T(8,128)S(1)} fusion(f32[2,512,384]{2,1,0:T(8,128)S(1)} %bitcast_dynamic-update-slice_fusion.5, s32[]{:T(128)S(6)} %select_n.162, f32[1,512,384]{2,1,0:T(8,128)S(1)} %constant_dynamic-slice_fusion.9, bf16[512,384]{1,0:T(8,128)(2,1)S(1)} %collective-permute-done.2, ...), kind=kOutput, calls=%fused_computation.35 | convolution fusion | flops 203358208 | bytes 2494480 | tf_op jit(solution)/shard_map/dot_general | solution.py:73
  147.2 2.3 %bitcast_dynamic-update-slice_fusion.3 = f32[2,512,384]{2,1,0:T(8,128)S(1)} fusion(f32[2,512,384]{2,1,0:T(8,128)S(1)} %bitcast_dynamic-update-slice_fusion.4, s32[]{:T(128)S(6)} %select_n.170, f32[1,512,384]{2,1,0:T(8,128)S(1)} %constant_dynamic-slice_fusion.5, bf16[512,384]{1,0:T(8,128)(2,1)S(1)} %collective-permute-done.3, ...), kind=kOutput, calls=%fused_computation.33 | convolution fusion | flops 203358208 | bytes 2494480 | tf_op jit(solution)/shard_map/dot_general | solution.py:73
  149.4 3.3 %collective-permute-done.4 = bf16[512,384]{1,0:T(8,128)(2,1)S(1)} collective-permute-done((bf16[512,384]{1,0:T(8,128)(2,1)S(1)}, bf16[512,384]{1,0:T(8,128)(2,1)S(1)}, u32[]{:S(2)}, u32[]{:S(2)}) %collective-permute-start.4) | collective-permute-done | bytes 393248 | tf_op jit(solution)/shard_map/ppermute | solution.py:10
  152.8 0.1 broadcast.17.clone.1
  153.0 1.6 collective-permute-done.5
  154.6 0.1 bitcast_dynamic-update-slice_fusion.2
  154.8 16.5 %collective-permute-done.6 = bf16[512,384]{1,0:T(8,128)(2,1)S(1)} collective-permute-done((bf16[512,384]{1,0:T(8,128)(2,1)S(1)}, bf16[512,384]{1,0:T(8,128)(2,1)S(1)}, u32[]{:S(2)}, u32[]{:S(2)}) %collective-permute-start.6) | collective-permute-done | bytes 393248 | tf_op jit(solution)/shard_map/ppermute | solution.py:10
  171.3 0.1 bitcast_dynamic-update-slice_fusion.1
  171.5 0.1 bitcast_dynamic-update-slice_fusion
  171.6 1.1 copy-done.2
  (37 shorter events, 0.6 us)
Async XLA Ops:
  7.2 53.7 %copy-start = (bf16[2,512,384]{2,1,0:T(8,128)(2,1)S(1)}, bf16[2,512,384]{2,1,0:T(8,128)(2,1)}, u32[]{:S(2)}) copy-start(bf16[2,512,384]{2,1,0:T(8,128)(2,1)} %param.9) | copy-start | bytes 2359300
  7.2 112.1 %all-reduce.3.cloned.1.call-start = ((), (), s32[]{:S(2)}) async-start(), calls=%async_computation | async-start | bytes 4194304 | tf_op jit(solution)/shard_map/psum | solution.py:71
  24.1 36.8 %collective-permute-start = (bf16[512,384]{1,0:T(8,128)(2,1)}, bf16[512,384]{1,0:T(8,128)(2,1)S(1)}, u32[]{:S(2)}, u32[]{:S(2)}) collective-permute-start(bf16[512,384]{1,0:T(8,128)(2,1)} %get-tuple-element.24), channel_id=1, source_target_pairs={{28,0},{0,4},{4,8},{8,12},{12,16},{16,20},{20,24},{24,28},{29,1},{... | collective-permute-start | bytes 1179656 | tf_op jit(solution)/shard_map/ppermute | solution.py:10
  26.9 35.2 %collective-permute-start.1 = (bf16[512,384]{1,0:T(8,128)(2,1)S(1)}, bf16[512,384]{1,0:T(8,128)(2,1)S(1)}, u32[]{:S(2)}, u32[]{:S(2)}) collective-permute-start(bf16[512,384]{1,0:T(8,128)(2,1)S(1)} %get-tuple-element.23), channel_id=1, source_target_pairs={{20,0},{24,4},{28,8},{0,12},{4,16},{8,20},{12,24},{16,28},{21,1},{... | collective-permute-start | bytes 1179656 | tf_op jit(solution)/shard_map/ppermute | solution.py:10
  29.6 33.9 %collective-permute-start.2 = (bf16[512,384]{1,0:T(8,128)(2,1)S(1)}, bf16[512,384]{1,0:T(8,128)(2,1)S(1)}, u32[]{:S(2)}, u32[]{:S(2)}) collective-permute-start(bf16[512,384]{1,0:T(8,128)(2,1)S(1)} %get-tuple-element.25), channel_id=1, source_target_pairs={{12,0},{16,4},{20,8},{24,12},{28,16},{0,20},{4,24},{8,28},{13,1},{... | collective-permute-start | bytes 1179656 | tf_op jit(solution)/shard_map/ppermute | solution.py:10
  30.8 34.0 %collective-permute-start.3 = (bf16[512,384]{1,0:T(8,128)(2,1)S(1)}, bf16[512,384]{1,0:T(8,128)(2,1)S(1)}, u32[]{:S(2)}, u32[]{:S(2)}) collective-permute-start(bf16[512,384]{1,0:T(8,128)(2,1)S(1)} %get-tuple-element.22), channel_id=1, source_target_pairs={{4,0},{8,4},{12,8},{16,12},{20,16},{24,20},{28,24},{0,28},{5,1},{9... | collective-permute-start | bytes 1179656 | tf_op jit(solution)/shard_map/ppermute | solution.py:10
  64.7 1.3 copy-start.3
  64.7 2.6 %copy-start.4 = (f32[16]{0:T(128)S(1)}, f32[16]{0:T(128)}, u32[]{:S(2)}) copy-start(f32[16]{0:T(128)} %param.11) | copy-start | bytes 196
  64.7 5.7 %copy-start.5 = (f32[16]{0:T(128)S(1)}, f32[16]{0:T(128)}, u32[]{:S(2)}) copy-start(f32[16]{0:T(128)} %param.12) | copy-start | bytes 196
  64.7 54.6 %copy-start.10 = (f32[512]{0:T(512)S(1)}, f32[512]{0:T(512)}, u32[]{:S(2)}) copy-start(f32[512]{0:T(512)} %param.14) | copy-start | bytes 6148
  64.7 54.6 %copy-start.11 = (f32[512]{0:T(512)S(1)}, f32[512]{0:T(512)}, u32[]{:S(2)}) copy-start(f32[512]{0:T(512)} %param.13) | copy-start | bytes 6148
  122.8 1.0 copy-start.9
  126.2 1.0 copy-start.8
  132.3 4.4 %copy-start.7 = (bf16[512,512]{1,0:T(8,128)(2,1)S(1)}, bf16[512,512]{1,0:T(8,128)(2,1)}, u32[]{:S(2)}) copy-start(bf16[512,512]{1,0:T(8,128)(2,1)} %get-tuple-element.20) | copy-start | bytes 1572868
  132.4 20.4 %collective-permute-start.4 = (bf16[512,384]{1,0:T(8,128)(2,1)S(1)}, bf16[512,384]{1,0:T(8,128)(2,1)S(1)}, u32[]{:S(2)}, u32[]{:S(2)}) collective-permute-start(bf16[512,384]{1,0:T(8,128)(2,1)S(1)} %convolution_convert_fusion.7), channel_id=1, source_target_pairs={{4,0},{8,4},{12,8},{16,12},{20,16},{24,20},{28,24},{0,28},{5,1},{9... | collective-permute-start | bytes 1179656 | tf_op jit(solution)/shard_map/ppermute | solution.py:10
  136.7 18.0 %collective-permute-start.5 = (bf16[512,384]{1,0:T(8,128)(2,1)S(1)}, bf16[512,384]{1,0:T(8,128)(2,1)S(1)}, u32[]{:S(2)}, u32[]{:S(2)}) collective-permute-start(bf16[512,384]{1,0:T(8,128)(2,1)S(1)} %convolution_convert_fusion.6), channel_id=1, source_target_pairs={{12,0},{16,4},{20,8},{24,12},{28,16},{0,20},{4,24},{8,28},{13,1},{... | collective-permute-start | bytes 1179656 | tf_op jit(solution)/shard_map/ppermute | solution.py:10
  136.7 5.6 %copy-start.6 = (bf16[512,512]{1,0:T(8,128)(2,1)S(1)}, bf16[512,512]{1,0:T(8,128)(2,1)}, u32[]{:S(2)}) copy-start(bf16[512,512]{1,0:T(8,128)(2,1)} %get-tuple-element.21) | copy-start | bytes 1572868
  139.2 32.1 %collective-permute-start.6 = (bf16[512,384]{1,0:T(8,128)(2,1)S(1)}, bf16[512,384]{1,0:T(8,128)(2,1)S(1)}, u32[]{:S(2)}, u32[]{:S(2)}) collective-permute-start(bf16[512,384]{1,0:T(8,128)(2,1)S(1)} %convolution_convert_fusion.5), channel_id=1, source_target_pairs={{20,0},{24,4},{28,8},{0,12},{4,16},{8,20},{12,24},{16,28},{21,1},{... | collective-permute-start | bytes 1179656 | tf_op jit(solution)/shard_map/ppermute | solution.py:10
  144.6 26.8 %collective-permute-start.7 = (bf16[512,384]{1,0:T(8,128)(2,1)S(1)}, bf16[512,384]{1,0:T(8,128)(2,1)S(1)}, u32[]{:S(2)}, u32[]{:S(2)}) collective-permute-start(bf16[512,384]{1,0:T(8,128)(2,1)S(1)} %convolution_convert_fusion.4), channel_id=1, source_target_pairs={{28,0},{0,4},{4,8},{8,12},{12,16},{16,20},{20,24},{24,28},{29,1},{... | collective-permute-start | bytes 1179656 | tf_op jit(solution)/shard_map/ppermute | solution.py:10
  149.4 3.6 %copy-start.1 = (f32[2,512,384]{2,1,0:T(8,128)}, f32[2,512,384]{2,1,0:T(8,128)S(1)}, u32[]{:S(2)}) copy-start(f32[2,512,384]{2,1,0:T(8,128)S(1)} %bitcast_dynamic-update-slice_fusion.3) | copy-start | bytes 4718596
  171.5 1.1 copy-start.2
Sparse Core Ops, SparseCore 0:
  66.2 53.0 all-reduce.2
where the time goes:
time: 180 us
  waiting for transfers between devices  92.8 us (52%)
  matrix products  25.6 us (14%)
  between operations  19.4 us (11%)
  starting transfers between devices  16.2 us (9%)
  other arithmetic  14.2 us (8%)
  local copies, waits for them, and re-layouts  11.4 us (6%)
    ppermute x8, waiting for transfers between devices, passed_along(): return lax.ppermute(block, axis, route)  47.1 us
    psum x1, waiting for transfers between devices, shards(): lax.psum(partial_values.astype(jnp.bfloat16), 'aux').astype(jnp.float32)  45.7 us
    ppermute x8, starting transfers between devices, passed_along(): return lax.ppermute(block, axis, route)  16.1 us
    dot_general x4, matrix products, shards(): lax.dot_general(amplitude, block_i, (((0,), (0,)), ((), ())), preferred_e...  11.1 us
    dot_general x4, matrix products, shards(): term_alpha = jnp.dot(amplitude, block_j, preferred_element_type=jnp.float32)  9.44 us
    reduce_sum x1, other arithmetic, stored_row(): return jnp.sum(jnp.where(row_orbital == orbital, places, 0))  6.46 us
    reduce_sum x2, other arithmetic, lookup(): jnp.sum(jnp.where(places == orbital, values_table, jnp.zeros_like(values_...  6.2 us
    dot_general x4, matrix products, shards(): lax.dot_general(block_i, block_j, contract, preferred_element_type=jnp.fl...  5.08 us
  transfers between devices with their start and end apart: 9, of which 5 were waited for; matrix products, arithmetic and copies ran while one was open for 12% of the time, Pallas kernels for 0%

commit v1 on v0

v1 whole, which is shorter than its diff:
```python
import functools

import jax
import jax.numpy as jnp
from jax import lax
from jax.experimental import pallas as pl
from jax.experimental.pallas import tpu as pltpu
from jax.sharding import PartitionSpec as P

MESH = pl.DeviceIdType.MESH


def kernel(
    workers,
    parts,
    slots,
    b_alpha,
    b_beta,
    eps_vir_alpha,
    eps_vir_beta,
    eps_occ_alpha,
    eps_occ_beta,
    row_orbital,
    pair_list,
    live_mask,
    gamma_alpha,
    gamma_beta,
    send_block,
    block_j,
    part_send,
    part_recv,
    amp,
    term_send,
    term_recv,
    fetch_sems,
    part_sems,
    amp_sems,
    term_sems,
):
    rows, nvir, cols = b_alpha.shape
    quarter = nvir // parts
    worker = lax.axis_index("occ")
    me = lax.axis_index("aux")
    distances = [1 + s * (workers // slots) for s in range(slots)]
    ahead = [lax.rem(worker + d, workers) for d in distances]
    behind = [lax.rem(worker + workers - d, workers) for d in distances]
    peers = [lax.rem(me + k, parts) for k in range(1, parts)]

    barrier = pltpu.get_barrier_semaphore()
    for target in ahead + behind:
        pl.semaphore_signal(barrier, inc=1, device_id={"occ": target}, device_id_type=MESH)
    for peer in peers:
        pl.semaphore_signal(barrier, inc=1, device_id={"aux": peer}, device_id_type=MESH)

    def local_row(label):
        found = jnp.int32(0)
        for r in range(rows):
            found = jnp.where(row_orbital[worker * rows + r] == label, r, found)
        return found

    row_i = [local_row(pair_list[s, worker, 0]) for s in range(slots)]
    row_out = [local_row(pair_list[s, ahead[s], 1]) for s in range(slots)]
    for s in range(slots):
        send_block[s] = b_beta[row_out[s]]
    pl.semaphore_wait(barrier, 2 * slots + parts - 1)

    def remote(src, dst, sems, index, where):
        return pltpu.make_async_remote_copy(
            src_ref=src,
            dst_ref=dst,
            send_sem=sems.at[(0,) + index],
            recv_sem=sems.at[(1,) + index],
            device_id=where,
            device_id_type=MESH,
        )

    fetches = [
        remote(send_block.at[s], block_j.at[s], fetch_sems, (s,), {"occ": ahead[s]})
        for s in range(slots)
    ]
    part_copies = [
        [
            remote(part_send.at[s, peers[k]], part_recv.at[s, k], part_sems, (s, k), {"aux": peers[k]})
            for k in range(parts - 1)
        ]
        for s in range(slots)
    ]
    amp_copies = [
        [
            remote(amp.at[s, me], amp.at[s, me], amp_sems, (s, k), {"aux": peers[k]})
            for k in range(parts - 1)
        ]
        for s in range(slots)
    ]
    returns = [
        remote(term_send.at[s], term_recv.at[s], term_sems, (s,), {"occ": behind[s]})
        for s in range(slots)
    ]
    for fetch in fetches:
        fetch.start()

    vir_row = eps_vir_alpha[pl.ds(me, 1), :]
    vir_gap = jnp.broadcast_to(vir_row, (quarter, quarter)).T[:, :1] + eps_vir_beta[...]

    def add_rows(totals, first, picked, term):
        for r in range(rows):
            share = jnp.where(picked == r, term, 0.0)
            totals[r] = share if first else totals[r] + share

    def sums(s):
        fetches[s].wait_recv()
        partial = lax.dot_general(
            b_alpha[row_i[s]],
            block_j[s],
            (((1,), (1,)), ((), ())),
            preferred_element_type=jnp.float32,
        )
        part_send[s] = partial.astype(jnp.bfloat16).reshape(parts, quarter, nvir)
        for copy in part_copies[s]:
            copy.start()

    def amplitude(s):
        total = part_send[s, me].astype(jnp.float32)
        for k in range(parts - 1):
            part_copies[s][k].wait_recv()
            total = total + part_recv[s, k].astype(jnp.float32)
        occ = eps_occ_alpha[pair_list[s, worker, 0]]
        occ_beta = eps_occ_beta[pair_list[s, worker, 1]]
        live = live_mask[s, worker].astype(jnp.float32)
        amp[s, me] = (live * total / (vir_gap - occ - occ_beta)).astype(jnp.bfloat16)
        for copy in amp_copies[s]:
            copy.start()

    def terms(s):
        for copy in amp_copies[s]:
            copy.wait_recv()
        whole = amp[s].reshape(nvir, nvir)
        term_send[s] = lax.dot_general(
            whole,
            b_alpha[row_i[s]],
            (((0,), (0,)), ((), ())),
            preferred_element_type=jnp.float32,
        ).astype(jnp.bfloat16)
        returns[s].start()
        add_rows(
            gamma_alpha,
            s == 0,
            row_i[s],
            jnp.dot(whole, block_j[s], preferred_element_type=jnp.float32),
        )

    def returned(s):
        returns[s].wait_recv()
        add_rows(gamma_beta, s == 0, row_out[s], term_recv[s].astype(jnp.float32))

    for s in range(slots):
        sums(s)
        if s >= 1:
            terms(s - 1)
        amplitude(s)
    terms(slots - 1)
    for s in range(slots):
        returned(s)
    for s in range(slots):
        fetches[s].wait_send()
        returns[s].wait_send()
        for copy in part_copies[s] + amp_copies[s]:
            copy.wait_send()


def solution(mesh):
    workers, parts = mesh.shape["occ"], mesh.shape["aux"]

    def shards(
        b_alpha,
        b_beta,
        eps_occ_alpha,
        eps_occ_beta,
        eps_vir_alpha,
        eps_vir_beta,
        row_orbital,
        pair_list,
        live_mask,
    ):
        rows, nvir, cols = b_alpha.shape
        slots = pair_list.shape[0]
        quarter = nvir // parts
        vmem = pl.BlockSpec(memory_space=pltpu.VMEM)
        smem = pl.BlockSpec(memory_space=pltpu.SMEM)
        gamma = jax.ShapeDtypeStruct((rows, nvir, cols), jnp.float32)
        block = pltpu.VMEM((slots, nvir, cols), jnp.bfloat16)
        return pl.pallas_call(
            functools.partial(kernel, workers, parts, slots),
            out_shape=(gamma, gamma),
            in_specs=[vmem] * 4 + [smem] * 5,
            out_specs=(vmem, vmem),
            scratch_shapes=[
                block,
                block,
                pltpu.VMEM((slots, parts, quarter, nvir), jnp.bfloat16),
                pltpu.VMEM((slots, parts - 1, quarter, nvir), jnp.bfloat16),
                pltpu.VMEM((slots, parts, quarter, nvir), jnp.bfloat16),
                block,
                block,
                pltpu.SemaphoreType.DMA((2, slots)),
                pltpu.SemaphoreType.DMA((2, slots, parts - 1)),
                pltpu.SemaphoreType.DMA((2, slots, parts - 1)),
                pltpu.SemaphoreType.DMA((2, slots)),
            ],
            compiler_params=pltpu.CompilerParams(
                collective_id=0, has_side_effects=True, vmem_limit_bytes=48 * 1024 * 1024
            ),
        )(
            b_alpha,
            b_beta,
            eps_vir_alpha.reshape(parts, quarter),
            eps_vir_beta.reshape(1, nvir),
            eps_occ_alpha,
            eps_occ_beta,
            row_orbital,
            pair_list,
            live_mask,
        )

    placed = (P("occ", None, "aux"), P("occ", None, "aux"), P(), P(), P(), P(), P(), P(), P())
    return jax.shard_map(
        shards,
        mesh=mesh,
        in_specs=placed,
        out_specs=(P("occ", None, "aux"), P("occ", None, "aux")),
        check_vma=False,
    )
```

time: 180 us -> 121 us (0.67)
  the two profiles are of different devices: /device:TPU:0 before, /device:TPU:9 now
where the time goes in v1:
time: 121 us; the launch traced here: 120 us
  Pallas kernels  110 us (91%)
  local copies, waits for them, and re-layouts  9.34 us (8%)
    pallas_call x1, Pallas kernels, shards(): pl.pallas_call(functools.partial(kernel, workers, parts, slots), out_shap...  110 us
    unnamed x19, local copies, waits for them, and re-layouts  9.34 us

profile of v1, /device:TPU:9, one launch (start us, length us, event | category | flops | bytes accessed | tf_op | source)
XLA Modules:
  0.0 120.3 jit_solution(2984779794496215412)
XLA Ops:
  0.6 0.8 copy.11.pair_list
  1.4 0.0 copy-start
  1.4 1.1 copy-done
  2.5 0.0 copy-start.1
  2.5 1.1 copy-done.1
  3.7 0.0 copy-start.2
  3.7 0.7 copy-done.2
  4.4 0.0 copy-start.3
  4.4 0.7 copy-done.3
  5.0 0.0 copy-start.4
  5.0 0.7 copy-done.4
  5.7 0.0 copy-start.5
  5.7 0.7 copy-done.5
  6.4 0.0 copy-start.6
  6.4 0.7 copy-done.6
  7.0 0.0 copy-start.7
  7.0 0.7 copy-done.7
  7.7 110.3 %shard_map.104 = (f32[2,512,384]{2,1,0:T(8,128)S(1)}, f32[2,512,384]{2,1,0:T(8,128)S(1)}) custom-call(bf16[2,512,384]{2,1,0:T(8,128)(2,1)S(1)} %copy-done, bf16[2,512,384]{2,1,0:T(8,128)(2,1)S(1)} %copy-done.1, f32[4,128]{1,0:T(4,128)S(1)} %bitcast.2, f32[1,512]{1,0:T(1,128)S(1)} %bitcast.3, f32[16]{0:T(128)S(1)} %copy-done.5, f32[16]{0:T(128)S(1)} %copy-done.6, ...), custom_call_target="tpu_custom_call" | custom-call | tf_op jit(solution)/shard_map/pallas_call | solution.py:192
  118.0 1.1 copy.14
  119.2 1.1 copy.15
Async XLA Ops:
  1.4 1.1 copy-start
  2.5 1.1 copy-start.1
  3.7 0.7 copy-start.2
  4.4 0.7 copy-start.3
  5.0 0.7 copy-start.4
  5.7 0.7 copy-start.5
  6.4 0.7 copy-start.6
  7.0 0.7 copy-start.7

commit v2 on v1

v2 whole, which is shorter than its diff:
```python
import functools

import jax
import jax.numpy as jnp
from jax import lax
from jax.experimental import pallas as pl
from jax.experimental.pallas import tpu as pltpu
from jax.sharding import PartitionSpec as P

MESH = pl.DeviceIdType.MESH


def kernel(
    workers,
    parts,
    slots,
    b_alpha_hbm,
    b_beta_hbm,
    vir_alpha_hbm,
    vir_beta_hbm,
    occ_alpha_hbm,
    occ_beta_hbm,
    row_orbital_hbm,
    pair_list_hbm,
    live_mask_hbm,
    gamma_alpha_hbm,
    gamma_beta_hbm,
    b_alpha,
    b_beta,
    eps_vir_alpha,
    eps_vir_beta,
    eps_occ_alpha,
    eps_occ_beta,
    row_orbital,
    pair_list,
    live_mask,
    gamma_alpha,
    gamma_beta,
    send_block,
    block_j,
    half_send,
    half_recv,
    cross_send,
    cross_recv,
    amp,
    term_send,
    term_recv,
    in_sems,
    out_sems,
    fetch_sems,
    half_sems,
    cross_sems,
    pair_sems,
    far_sems,
    forward_sems,
    term_sems,
):
    rows, nvir, cols = b_alpha.shape
    chips = parts // 2
    quarter = nvir // parts
    worker = lax.axis_index("occ")
    me = lax.axis_index("aux")
    chip, core = me // 2, lax.rem(me, 2)
    partner = me + 1 - 2 * core
    distances = [1 + s * (workers // slots) for s in range(slots)]
    ahead = [lax.rem(worker + d, workers) for d in distances]
    behind = [lax.rem(worker + workers - d, workers) for d in distances]
    others = [lax.rem(chip + k, chips) for k in range(1, chips)]
    sources = [lax.rem(chip + chips - k, chips) for k in range(1, chips)]

    loads = [
        pltpu.make_async_copy(src, dst, in_sems.at[n])
        for n, (src, dst) in enumerate(
            [
                (b_beta_hbm, b_beta),
                (row_orbital_hbm, row_orbital),
                (pair_list_hbm, pair_list),
                (live_mask_hbm, live_mask),
                (occ_alpha_hbm, eps_occ_alpha),
                (occ_beta_hbm, eps_occ_beta),
                (vir_alpha_hbm, eps_vir_alpha),
                (vir_beta_hbm, eps_vir_beta),
                (b_alpha_hbm, b_alpha),
            ]
        )
    ]
    for load in loads:
        load.start()
    barrier = pltpu.get_barrier_semaphore()
    for target in ahead + behind:
        pl.semaphore_signal(barrier, inc=1, device_id={"occ": target}, device_id_type=MESH)
    for peer in [partner] + [other * 2 + core for other in others]:
        pl.semaphore_signal(barrier, inc=1, device_id={"aux": peer}, device_id_type=MESH)
    for load in loads[:3]:
        load.wait()

    def local_row(label):
        found = jnp.int32(0)
        for r in range(rows):
            found = jnp.where(row_orbital[worker * rows + r] == label, r, found)
        return found

    row_i = [local_row(pair_list[s, 0, worker]) for s in range(slots)]
    row_out = [local_row(pair_list[s, 1, ahead[s]]) for s in range(slots)]
    for s in range(slots):
        send_block[s] = b_beta[row_out[s]]
    pl.semaphore_wait(barrier, 2 * slots + chips)

    def remote(src, dst, sems, index, where):
        return pltpu.make_async_remote_copy(
            src_ref=src,
            dst_ref=dst,
            send_sem=sems.at[(0,) + index],
            recv_sem=sems.at[(1,) + index],
            device_id=where,
            device_id_type=MESH,
        )

    each = range(slots)
    hops = range(chips - 1)
    fetches = [
        remote(send_block.at[s], block_j.at[s], fetch_sems, (s,), {"occ": ahead[s]}) for s in each
    ]
    halves = [
        remote(half_send.at[s, 1 - core], half_recv.at[s], half_sems, (s,), {"aux": partner})
        for s in each
    ]
    crosses = [
        [
            remote(
                cross_send.at[s, k], cross_recv.at[s, k], cross_sems, (s, k),
                {"aux": others[k] * 2 + core},
            )
            for k in hops
        ]
        for s in each
    ]
    nears = [
        remote(amp.at[s, core, chip], amp.at[s, core, chip], pair_sems, (s,), {"aux": partner})
        for s in each
    ]
    fars = [
        [
            remote(
                amp.at[s, core, chip], amp.at[s, core, chip], far_sems, (s, k),
                {"aux": others[k] * 2 + core},
            )
            for k in hops
        ]
        for s in each
    ]
    forwards = [
        [
            remote(
                amp.at[s, core, sources[k]], amp.at[s, core, sources[k]], forward_sems, (s, k),
                {"aux": partner},
            )
            for k in hops
        ]
        for s in each
    ]
    returns = [
        remote(term_send.at[s], term_recv.at[s], term_sems, (s,), {"occ": behind[s]}) for s in each
    ]
    for fetch in fetches:
        fetch.start()
    for load in loads[3:]:
        load.wait()

    vir_row = eps_vir_alpha[pl.ds(core * chips + chip, 1), :]
    vir_gap = jnp.broadcast_to(vir_row, (quarter, quarter)).T[:, :1] + eps_vir_beta[...]

    def add_row(totals, first, r, picked, term):
        share = jnp.where(picked == r, term, 0.0)
        totals[r] = share if first else totals[r] + share

    def sums(s):
        fetches[s].wait_recv()
        partial = lax.dot_general(
            b_alpha[row_i[s]],
            block_j[s],
            (((1,), (1,)), ((), ())),
            preferred_element_type=jnp.float32,
        )
        half_send[s] = partial.astype(jnp.bfloat16).reshape(2, chips, quarter, nvir)
        halves[s].start()

    def pair_sum(s, owner):
        return half_send[s, core, owner].astype(jnp.float32) + half_recv[s, owner].astype(jnp.float32)

    def crossing(s):
        halves[s].wait_recv()
        for k in hops:
            cross_send[s, k] = pair_sum(s, others[k]).astype(jnp.bfloat16)
            crosses[s][k].start()

    def amplitude(s):
        total = pair_sum(s, chip)
        for k in hops:
            crosses[s][k].wait_recv()
            total = total + cross_recv[s, k].astype(jnp.float32)
        occ_alpha = eps_occ_alpha[pair_list[s, 0, worker]]
        occ_beta = eps_occ_beta[pair_list[s, 1, worker]]
        live = live_mask[s, worker].astype(jnp.float32)
        amp[s, core, chip] = (live * total / (vir_gap - occ_alpha - occ_beta)).astype(jnp.bfloat16)
        for copy in fars[s]:
            copy.start()
        nears[s].start()

    def forward(s):
        for k in hops:
            fars[s][k].wait_recv()
            forwards[s][k].start()

    def terms(s):
        nears[s].wait_recv()
        for copy in forwards[s]:
            copy.wait_recv()
        whole = amp[s].reshape(nvir, nvir)
        term_send[s] = lax.dot_general(
            whole,
            b_alpha[row_i[s]],
            (((0,), (0,)), ((), ())),
            preferred_element_type=jnp.float32,
        ).astype(jnp.bfloat16)
        returns[s].start()
        term = jnp.dot(whole, block_j[s], preferred_element_type=jnp.float32)
        for r in range(rows):
            add_row(gamma_alpha, s == 0, r, row_i[s], term)

    for s in each:
        sums(s)
        if s >= 1:
            forward(s - 1)
        crossing(s)
        if s >= 1:
            terms(s - 1)
        amplitude(s)
    forward(slots - 1)
    terms(slots - 1)
    stores = [
        pltpu.make_async_copy(src.at[r], dst.at[r], out_sems.at[n, r])
        for n, (src, dst) in enumerate(
            [(gamma_alpha, gamma_alpha_hbm), (gamma_beta, gamma_beta_hbm)]
        )
        for r in range(rows)
    ]
    for r in range(rows):
        stores[r].start()
    for s in each:
        returns[s].wait_recv()
        for r in range(rows):
            add_row(gamma_beta, s == 0, r, row_out[s], term_recv[s].astype(jnp.float32))
            if s == slots - 1:
                stores[rows + r].start()
    for s in each:
        for copy in [fetches[s], halves[s], nears[s], returns[s]]:
            copy.wait_send()
        for copy in crosses[s] + fars[s] + forwards[s]:
            copy.wait_send()
    for store in stores:
        store.wait()


def solution(mesh):
    workers, parts = mesh.shape["occ"], mesh.shape["aux"]

    def shards(
        b_alpha,
        b_beta,
        eps_occ_alpha,
        eps_occ_beta,
        eps_vir_alpha,
        eps_vir_beta,
        row_orbital,
        pair_list,
        live_mask,
    ):
        rows, nvir, cols = b_alpha.shape
        slots = pair_list.shape[0]
        quarter = nvir // parts
        chips = parts // 2
        hbm = pl.BlockSpec(memory_space=pltpu.HBM)
        gamma = jax.ShapeDtypeStruct((rows, nvir, cols), jnp.float32)
        block = pltpu.VMEM((slots, nvir, cols), jnp.bfloat16)
        piece = (quarter, nvir)
        copies = pltpu.SemaphoreType.DMA((2, slots))
        hop_copies = pltpu.SemaphoreType.DMA((2, slots, chips - 1))
        pairs = jnp.transpose(pair_list, (0, 2, 1))
        return pl.pallas_call(
            functools.partial(kernel, workers, parts, slots),
            out_shape=(gamma, gamma),
            in_specs=[hbm] * 9,
            out_specs=(hbm, hbm),
            scratch_shapes=[
                pltpu.VMEM(b_alpha.shape, b_alpha.dtype),
                pltpu.VMEM(b_beta.shape, b_beta.dtype),
                pltpu.VMEM((parts, quarter), jnp.float32),
                pltpu.VMEM((1, nvir), jnp.float32),
                pltpu.SMEM(eps_occ_alpha.shape, jnp.float32),
                pltpu.SMEM(eps_occ_beta.shape, jnp.float32),
                pltpu.SMEM(row_orbital.shape, jnp.int32),
                pltpu.SMEM(pairs.shape, jnp.int32),
                pltpu.SMEM(live_mask.shape, jnp.int32),
                pltpu.VMEM(gamma.shape, jnp.float32),
                pltpu.VMEM(gamma.shape, jnp.float32),
                block,
                block,
                pltpu.VMEM((slots, 2, chips) + piece, jnp.bfloat16),
                pltpu.VMEM((slots, chips) + piece, jnp.bfloat16),
                pltpu.VMEM((slots, chips - 1) + piece, jnp.bfloat16),
                pltpu.VMEM((slots, chips - 1) + piece, jnp.bfloat16),
                pltpu.VMEM((slots, 2, chips) + piece, jnp.bfloat16),
                block,
                block,
                pltpu.SemaphoreType.DMA((9,)),
                pltpu.SemaphoreType.DMA((2, rows)),
                copies,
                copies,
                hop_copies,
                copies,
                hop_copies,
                hop_copies,
                copies,
            ],
            compiler_params=pltpu.CompilerParams(
                collective_id=0, has_side_effects=True, vmem_limit_bytes=56 * 1024 * 1024
            ),
        )(
            b_alpha,
            b_beta,
            eps_vir_alpha.reshape(parts, quarter),
            eps_vir_beta.reshape(1, nvir),
            eps_occ_alpha,
            eps_occ_beta,
            row_orbital,
            pairs,
            live_mask,
        )

    placed = (P("occ", None, "aux"), P("occ", None, "aux"), P(), P(), P(), P(), P(), P(), P())
    return jax.shard_map(
        shards,
        mesh=mesh,
        in_specs=placed,
        out_specs=(P("occ", None, "aux"), P("occ", None, "aux")),
        check_vma=False,
    )
```

time: 121 us -> 104 us (0.86)
  the two profiles are of different devices: /device:TPU:9 before, /device:TPU:0 now
where the time goes in v2:
time: 104 us
  Pallas kernels  99.3 us (95%)
  local copies, waits for them, and re-layouts  3.92 us (4%)
    pallas_call x1, Pallas kernels, shards(): pl.pallas_call(functools.partial(kernel, workers, parts, slots), out_shap...  99.3 us
    unnamed x4, local copies, waits for them, and re-layouts  3.92 us

profile of v2, /device:TPU:0, one launch (start us, length us, event | category | flops | bytes accessed | tf_op | source)
XLA Modules:
  0.0 103.9 jit_solution(757952616273465430)
XLA Ops:
  0.6 99.3 %shard_map.104 = (f32[2,512,384]{2,1,0:T(8,128)}, f32[2,512,384]{2,1,0:T(8,128)}) custom-call(bf16[2,512,384]{2,1,0:T(8,128)(2,1)} %b_alpha_hbm.1, bf16[2,512,384]{2,1,0:T(8,128)(2,1)} %b_beta_hbm.1, f32[4,128]{1,0:T(4,128)} %bitcast.4, f32[1,512]{1,0:T(1,128)} %bitcast.5, f32[16]{0:T(128)} %occ_alpha_hbm.1, f32[16]{0:T(128)} %occ_beta_hbm.1, ...), custom_call_target="tpu_custom_call" | custom-call | tf_op jit(solution)/shard_map/pallas_call | solution.py:290
  100.0 0.0 copy-start
  100.0 2.8 %copy.13 = f32[2,512,384]{2,1,0:T(8,128)} copy(f32[2,512,384]{2,1,0:T(8,128)} %get-tuple-element.4) | data formatting | bytes 3145728
  102.7 0.0 copy-done
  102.7 1.1 %copy.14 = f32[2,512,384]{2,1,0:T(8,128)} copy(f32[2,512,384]{2,1,0:T(8,128)S(1)} %copy-done) | data formatting | bytes 3145728
Async XLA Ops:
  100.0 2.8 %copy-start = (f32[2,512,384]{2,1,0:T(8,128)S(1)}, f32[2,512,384]{2,1,0:T(8,128)}, u32[]{:S(2)}) copy-start(f32[2,512,384]{2,1,0:T(8,128)} %get-tuple-element.5) | copy-start | bytes 4718596

commit v3 on v2

v3 whole, which is shorter than its diff:
```python
import functools

import jax
import jax.numpy as jnp
from jax import lax
from jax.experimental import pallas as pl
from jax.experimental.pallas import tpu as pltpu
from jax.sharding import PartitionSpec as P

MESH = pl.DeviceIdType.MESH


def kernel(
    workers,
    parts,
    slots,
    chunks,
    b_alpha_hbm,
    b_beta_hbm,
    vir_alpha_hbm,
    vir_beta_hbm,
    occ_alpha_hbm,
    occ_beta_hbm,
    row_orbital_hbm,
    pair_list_hbm,
    live_mask_hbm,
    gamma_alpha,
    gamma_beta,
    b_alpha,
    b_beta,
    eps_vir_alpha,
    eps_vir_beta,
    eps_occ_alpha,
    eps_occ_beta,
    row_orbital,
    pair_list,
    live_mask,
    send_block,
    block_j,
    half_send,
    half_recv,
    cross_send,
    cross_recv,
    amp,
    term_send,
    term_recv,
    in_sems,
    fetch_sems,
    half_sems,
    cross_sems,
    pair_sems,
    far_sems,
    forward_sems,
    term_sems,
):
    rows, nvir, cols = b_alpha.shape
    chips = parts // 2
    quarter = nvir // parts
    width = nvir // chunks
    worker = lax.axis_index("occ")
    me = lax.axis_index("aux")
    chip, core = me // 2, lax.rem(me, 2)
    partner = me + 1 - 2 * core
    distances = [1 + s * (workers // slots) for s in range(slots)]
    ahead = [lax.rem(worker + d, workers) for d in distances]
    behind = [lax.rem(worker + workers - d, workers) for d in distances]
    others = [lax.rem(chip + k, chips) for k in range(1, chips)]
    sources = [lax.rem(chip + chips - k, chips) for k in range(1, chips)]

    loads = [
        pltpu.make_async_copy(src, dst, in_sems.at[n])
        for n, (src, dst) in enumerate(
            [
                (b_beta_hbm, b_beta),
                (row_orbital_hbm, row_orbital),
                (pair_list_hbm, pair_list),
                (live_mask_hbm, live_mask),
                (occ_alpha_hbm, eps_occ_alpha),
                (occ_beta_hbm, eps_occ_beta),
                (vir_alpha_hbm, eps_vir_alpha),
                (vir_beta_hbm, eps_vir_beta),
                (b_alpha_hbm, b_alpha),
            ]
        )
    ]
    for load in loads:
        load.start()
    barrier = pltpu.get_barrier_semaphore()
    for target in ahead + behind:
        pl.semaphore_signal(barrier, inc=1, device_id={"occ": target}, device_id_type=MESH)
    for peer in [partner] + [other * 2 + core for other in others]:
        pl.semaphore_signal(barrier, inc=1, device_id={"aux": peer}, device_id_type=MESH)
    for load in loads[:3]:
        load.wait()

    def local_row(label):
        found = jnp.int32(0)
        for r in range(rows):
            found = jnp.where(row_orbital[worker * rows + r] == label, r, found)
        return found

    row_i = [local_row(pair_list[s, 0, worker]) for s in range(slots)]
    row_out = [local_row(pair_list[s, 1, ahead[s]]) for s in range(slots)]
    for s in range(slots):
        send_block[s] = b_beta[row_out[s]]
    pl.semaphore_wait(barrier, 2 * slots + chips)

    def remote(src, dst, sems, index, where):
        return pltpu.make_async_remote_copy(
            src_ref=src,
            dst_ref=dst,
            send_sem=sems.at[(0,) + index],
            recv_sem=sems.at[(1,) + index],
            device_id=where,
            device_id_type=MESH,
        )

    each = range(slots)
    hops = range(chips - 1)
    steps = range(chunks)
    spans = [pl.ds(c * width, width) for c in steps]
    fetches = [
        [
            remote(
                send_block.at[s, spans[c]], block_j.at[s, spans[c]], fetch_sems, (c, s),
                {"occ": ahead[s]},
            )
            for s in each
        ]
        for c in steps
    ]
    halves = [
        remote(half_send.at[c, 1 - core], half_recv.at[c], half_sems, (c,), {"aux": partner})
        for c in steps
    ]
    crosses = [
        [
            remote(
                cross_send.at[c, k], cross_recv.at[c, k], cross_sems, (c, k),
                {"aux": others[k] * 2 + core},
            )
            for k in hops
        ]
        for c in steps
    ]
    nears = [
        remote(amp.at[c, core, chip], amp.at[c, core, chip], pair_sems, (c,), {"aux": partner})
        for c in steps
    ]
    fars = [
        [
            remote(
                amp.at[c, core, chip], amp.at[c, core, chip], far_sems, (c, k),
                {"aux": others[k] * 2 + core},
            )
            for k in hops
        ]
        for c in steps
    ]
    forwards = [
        [
            remote(
                amp.at[c, core, sources[k]], amp.at[c, core, sources[k]], forward_sems, (c, k),
                {"aux": partner},
            )
            for k in hops
        ]
        for c in steps
    ]
    returns = [
        [
            remote(
                term_send.at[s, spans[c]], term_recv.at[s, spans[c]], term_sems, (c, s),
                {"occ": behind[s]},
            )
            for s in each
        ]
        for c in steps
    ]
    for c in steps:
        for s in each:
            fetches[c][s].start()
    for load in loads[3:]:
        load.wait()

    vir_row = eps_vir_alpha[pl.ds(core * chips + chip, 1), :]
    vir_column = jnp.broadcast_to(vir_row, (quarter, quarter)).T[:, :1]

    def sums(c):
        for s in each:
            fetches[c][s].wait_recv()
            partial = lax.dot_general(
                b_alpha[row_i[s]],
                block_j[s, spans[c]],
                (((1,), (1,)), ((), ())),
                preferred_element_type=jnp.float32,
            )
            half_send[c, :, :, s] = partial.astype(jnp.bfloat16).reshape(2, chips, quarter, width)
        halves[c].start()

    def pair_sum(c, owner):
        return half_send[c, core, owner].astype(jnp.float32) + half_recv[c, owner].astype(jnp.float32)

    def crossing(c):
        halves[c].wait_recv()
        for k in hops:
            cross_send[c, k] = pair_sum(c, others[k]).astype(jnp.bfloat16)
            crosses[c][k].start()

    def amplitude(c):
        total = pair_sum(c, chip)
        for k in hops:
            crosses[c][k].wait_recv()
            total = total + cross_recv[c, k].astype(jnp.float32)
        gap = vir_column + eps_vir_beta[:, spans[c]]
        for s in each:
            occ_alpha = eps_occ_alpha[pair_list[s, 0, worker]]
            occ_beta = eps_occ_beta[pair_list[s, 1, worker]]
            live = live_mask[s, worker].astype(jnp.float32)
            value = live * total[s] / (gap - occ_alpha - occ_beta)
            amp[c, core, chip, s] = value.astype(jnp.bfloat16)
        for copy in fars[c]:
            copy.start()
        nears[c].start()

    def forward(c):
        for k in hops:
            fars[c][k].wait_recv()
            forwards[c][k].start()

    def terms(c):
        nears[c].wait_recv()
        for copy in forwards[c]:
            copy.wait_recv()
        for s in each:
            term_send[s, spans[c]] = lax.dot_general(
                amp[c, :, :, s].reshape(nvir, width),
                b_alpha[row_i[s]],
                (((0,), (0,)), ((), ())),
                preferred_element_type=jnp.float32,
            ).astype(jnp.bfloat16)
            returns[c][s].start()

    for c in steps:
        sums(c)
        if c >= 1:
            forward(c - 1)
        crossing(c)
        if c >= 1:
            terms(c - 1)
        amplitude(c)
    forward(chunks - 1)
    terms(chunks - 1)
    for s in each:
        whole = jnp.concatenate([amp[c, :, :, s].reshape(nvir, width) for c in steps], axis=1)
        term = jnp.dot(whole, block_j[s], preferred_element_type=jnp.float32)
        for r in range(rows):
            share = jnp.where(row_i[s] == r, term, 0.0)
            gamma_alpha[r] = share if s == 0 else gamma_alpha[r] + share
    for c in steps:
        for s in each:
            returns[c][s].wait_recv()
        for r in range(rows):
            total = jnp.where(row_out[0] == r, term_recv[0, spans[c]].astype(jnp.float32), 0.0)
            for s in range(1, slots):
                total = total + jnp.where(
                    row_out[s] == r, term_recv[s, spans[c]].astype(jnp.float32), 0.0
                )
            gamma_beta[r, spans[c]] = total
    for c in steps:
        for copy in fetches[c] + [halves[c], nears[c]] + returns[c]:
            copy.wait_send()
        for copy in crosses[c] + fars[c] + forwards[c]:
            copy.wait_send()


def solution(mesh):
    workers, parts = mesh.shape["occ"], mesh.shape["aux"]

    def shards(
        b_alpha,
        b_beta,
        eps_occ_alpha,
        eps_occ_beta,
        eps_vir_alpha,
        eps_vir_beta,
        row_orbital,
        pair_list,
        live_mask,
    ):
        rows, nvir, cols = b_alpha.shape
        slots = pair_list.shape[0]
        quarter = nvir // parts
        chips = parts // 2
        vmem = pl.BlockSpec(memory_space=pltpu.VMEM)
        hbm = pl.BlockSpec(memory_space=pltpu.HBM)
        gamma = jax.ShapeDtypeStruct((rows, nvir, cols), jnp.float32)
        block = pltpu.VMEM((slots, nvir, cols), jnp.bfloat16)
        chunks = max(1, nvir // 128)
        piece = (slots, quarter, nvir // chunks)
        block_copies = pltpu.SemaphoreType.DMA((2, chunks, slots))
        copies = pltpu.SemaphoreType.DMA((2, chunks))
        hop_copies = pltpu.SemaphoreType.DMA((2, chunks, chips - 1))
        pairs = jnp.transpose(pair_list, (0, 2, 1))
        return pl.pallas_call(
            functools.partial(kernel, workers, parts, slots, chunks),
            out_shape=(gamma, gamma),
            in_specs=[hbm] * 9,
            out_specs=(vmem, vmem),
            scratch_shapes=[
                pltpu.VMEM(b_alpha.shape, b_alpha.dtype),
                pltpu.VMEM(b_beta.shape, b_beta.dtype),
                pltpu.VMEM((parts, quarter), jnp.float32),
                pltpu.VMEM((1, nvir), jnp.float32),
                pltpu.SMEM(eps_occ_alpha.shape, jnp.float32),
                pltpu.SMEM(eps_occ_beta.shape, jnp.float32),
                pltpu.SMEM(row_orbital.shape, jnp.int32),
                pltpu.SMEM(pairs.shape, jnp.int32),
                pltpu.SMEM(live_mask.shape, jnp.int32),
                block,
                block,
                pltpu.VMEM((chunks, 2, chips) + piece, jnp.bfloat16),
                pltpu.VMEM((chunks, chips) + piece, jnp.bfloat16),
                pltpu.VMEM((chunks, chips - 1) + piece, jnp.bfloat16),
                pltpu.VMEM((chunks, chips - 1) + piece, jnp.bfloat16),
                pltpu.VMEM((chunks, 2, chips) + piece, jnp.bfloat16),
                block,
                block,
                pltpu.SemaphoreType.DMA((9,)),
                block_copies,
                copies,
                hop_copies,
                copies,
                hop_copies,
                hop_copies,
                block_copies,
            ],
            compiler_params=pltpu.CompilerParams(
                collective_id=0, has_side_effects=True, vmem_limit_bytes=56 * 1024 * 1024
            ),
        )(
            b_alpha,
            b_beta,
            eps_vir_alpha.reshape(parts, quarter),
            eps_vir_beta.reshape(1, nvir),
            eps_occ_alpha,
            eps_occ_beta,
            row_orbital,
            pairs,
            live_mask,
        )

    placed = (P("occ", None, "aux"), P("occ", None, "aux"), P(), P(), P(), P(), P(), P(), P())
    return jax.shard_map(
        shards,
        mesh=mesh,
        in_specs=placed,
        out_specs=(P("occ", None, "aux"), P("occ", None, "aux")),
        check_vma=False,
    )
```

time: 104 us -> 84.9 us (0.82)
  Pallas kernels: 99.3 us -> 79.9 us
    pallas_call x1, Pallas kernels: 99.3 us -> 79.9 us  [shards(): pl.pallas_call(functools.partial(kernel, workers, parts, slots, chunks),...]
where the time goes in v3:
time: 84.9 us; the launch traced here: 84.4 us
  Pallas kernels  79.9 us (94%)
  local copies, waits for them, and re-layouts  3.92 us (5%)
    pallas_call x1, Pallas kernels, shards(): pl.pallas_call(functools.partial(kernel, workers, parts, slots, chunks),...  79.9 us
    unnamed x4, local copies, waits for them, and re-layouts  3.92 us

profile of v3, /device:TPU:0, one launch (start us, length us, event | category | flops | bytes accessed | tf_op | source)
XLA Modules:
  0.0 84.4 jit_solution(16879353817755687429)
XLA Ops:
  0.6 79.9 %shard_map.104 = (f32[2,512,384]{2,1,0:T(8,128)}, f32[2,512,384]{2,1,0:T(8,128)}) custom-call(bf16[2,512,384]{2,1,0:T(8,128)(2,1)} %b_alpha_hbm.1, bf16[2,512,384]{2,1,0:T(8,128)(2,1)} %b_beta_hbm.1, f32[4,128]{1,0:T(4,128)} %bitcast.4, f32[1,512]{1,0:T(1,128)} %bitcast.5, f32[16]{0:T(128)} %occ_alpha_hbm.1, f32[16]{0:T(128)} %occ_beta_hbm.1, ...), custom_call_target="tpu_custom_call" | custom-call | tf_op jit(solution)/shard_map/pallas_call | solution.py:305
  80.5 0.0 copy-start
  80.5 2.8 %copy.13 = f32[2,512,384]{2,1,0:T(8,128)} copy(f32[2,512,384]{2,1,0:T(8,128)} %get-tuple-element.4) | data formatting | bytes 3145728
  83.3 0.0 copy-done
  83.3 1.1 %copy.14 = f32[2,512,384]{2,1,0:T(8,128)} copy(f32[2,512,384]{2,1,0:T(8,128)S(1)} %copy-done) | data formatting | bytes 3145728
Async XLA Ops:
  80.5 2.8 %copy-start = (f32[2,512,384]{2,1,0:T(8,128)S(1)}, f32[2,512,384]{2,1,0:T(8,128)}, u32[]{:S(2)}) copy-start(f32[2,512,384]{2,1,0:T(8,128)} %get-tuple-element.5) | copy-start | bytes 4718596
